TPU v7x, 256 devices: a whole 4x4x8 slice. The times are simulated.
256 devices in a mesh: tm: 64 (over x, z, core), head: 4 (over y).
Axes of the slice: x: 4, y: 4, z: 8, core: 2. Of those that a mesh axis runs over, the one named last changes fastest.
Arguments:
- query_rows: float32 [32768, 2240], P('tm', 'head'), may hold values from -6 to 6
- key_rows: float32 [32768, 2240], P('tm', 'head'), may hold values from -6 to 6
- value_rows: float32 [32768, 2240], P('tm', 'head'), may hold values from -6 to 6
- out_weight: float32 [2240, 2240], P(None, 'head'), may hold values from -0.125 to 0.125
- cotangent: float32 [32768, 2240], P('tm', 'head'), may hold values from -6 to 6
Outputs:
- grad_query: float32 [32768, 2240], P('tm', 'head')
- grad_key: float32 [32768, 2240], P('tm', 'head')
- grad_value: float32 [32768, 2240], P('tm', 'head')
- grad_weight: float32 [2240, 2240], P('tm', 'head')
All inputs are finite; a program needn't handle non-finite values.
Results may differ from a plain program's by a relative error of at most 0.0003.
Values sent between devices are 32-bit elements; how exact they have to be, the bound alone decides.
No kernel may reach another device: no remote copies, remote signals or barrier semaphores. Data moves between devices by JAX's collectives and lax.ppermute only.
A program may use at most 128 MiB of HBM per device.

v0:
```python
import jax
import jax.numpy as jnp
from jax import lax
from jax.sharding import PartitionSpec as P

HEAD_DIM = 112


def prefix(part, axis, combine, identity, reverse):
    count = lax.axis_size(axis)
    place = lax.axis_index(axis)
    ahead = count - 1 - place if reverse else place
    gathered = jax.tree.map(lambda a: lax.all_gather(a, axis), part)
    state = jax.tree.map(lambda a, e: jnp.zeros_like(a) + jnp.asarray(e, a.dtype), part, identity)

    def one(lap, state):
        source = count - 1 - lap if reverse else lap
        return combine(
            state, jax.tree.map(lambda a: lax.dynamic_index_in_dim(a, source, 0, False), gathered)
        )

    return lax.fori_loop(0, ahead, one, state)


def add_pair(earlier, later):
    return (earlier[0] + later[0], earlier[1] + later[1])


def shards(query_rows, key_rows, value_rows, out_weight, cotangent):
    highest = lax.Precision.HIGHEST
    rows_here = query_rows.shape[0]
    width_here = query_rows.shape[1]
    heads_here = width_here // HEAD_DIM
    shape_heads = (rows_here, heads_here, HEAD_DIM)
    query_blk = query_rows.reshape(shape_heads)
    key_blk = key_rows.reshape(shape_heads)
    value_blk = value_rows.reshape(shape_heads)
    feat_q = jax.nn.relu(query_blk)
    feat_k = jax.nn.relu(key_blk)
    causal_mask = jnp.tril(jnp.ones((rows_here, rows_here), jnp.float32))
    local_state = jnp.einsum("thi,thj->hij", feat_k, value_blk, precision=highest)
    local_normal = jnp.sum(feat_k, axis=0)
    zero_state = jnp.zeros((heads_here, HEAD_DIM, HEAD_DIM), jnp.float32)
    zero_normal = jnp.zeros((heads_here, HEAD_DIM), jnp.float32)
    state, normal = prefix(
        (local_state, local_normal), "tm", add_pair, (zero_state, zero_normal), False
    )
    whole_grad = lax.all_gather(cotangent, "head", axis=1, tiled=True)
    grad_att = jnp.dot(
        whole_grad, out_weight, precision=highest, preferred_element_type=jnp.float32
    ).reshape(shape_heads)
    scores = jnp.einsum("thi,shi->hts", feat_q, feat_k, precision=highest) * causal_mask
    numer = jnp.einsum("hts,shj->thj", scores, value_blk, precision=highest)
    numer = numer + jnp.einsum("thi,hij->thj", feat_q, state, precision=highest)
    denom = (
        1.0
        + jnp.sum(scores, axis=-1).T
        + jnp.einsum("thi,hi->th", feat_q, normal, precision=highest)
    )
    attended = numer / denom[:, :, None]
    attended_flat = attended.reshape(rows_here, width_here)
    grad_num = grad_att / denom[:, :, None]
    grad_den = -jnp.sum(grad_att * attended, axis=-1) / denom
    local_back = jnp.einsum("thi,thj->hij", feat_q, grad_num, precision=highest)
    local_norm = jnp.einsum("th,thi->hi", grad_den, feat_q, precision=highest)
    back, back_norm = prefix(
        (local_back, local_norm), "tm", add_pair, (zero_state, zero_normal), True
    )
    grad_scores = (
        jnp.einsum("thj,shj->hts", grad_num, value_blk, precision=highest) + grad_den.T[:, :, None]
    ) * causal_mask
    grad_fq = jnp.einsum("hts,shi->thi", grad_scores, feat_k, precision=highest)
    grad_fq = (
        grad_fq
        + jnp.einsum("thj,hij->thi", grad_num, state, precision=highest)
        + grad_den[:, :, None] * normal[None]
    )
    grad_fk = jnp.einsum("hts,thi->shi", grad_scores, feat_q, precision=highest)
    grad_fk = (
        grad_fk + jnp.einsum("hij,shj->shi", back, value_blk, precision=highest) + back_norm[None]
    )
    grad_val = jnp.einsum("hts,thj->shj", scores, grad_num, precision=highest)
    grad_val = grad_val + jnp.einsum("shi,hij->shj", feat_k, back, precision=highest)
    grad_query = jnp.where(query_blk > 0, grad_fq, 0.0).reshape(rows_here, width_here)
    grad_key = jnp.where(key_blk > 0, grad_fk, 0.0).reshape(rows_here, width_here)
    grad_value = grad_val.reshape(rows_here, width_here)
    grad_weight = lax.psum_scatter(
        lax.dot_general(
            whole_grad,
            attended_flat,
            (((0,), (0,)), ((), ())),
            precision=highest,
            preferred_element_type=jnp.float32,
        ),
        "tm",
        scatter_dimension=0,
        tiled=True,
    )
    return (grad_query, grad_key, grad_value, grad_weight)


def solution(mesh):
    return jax.shard_map(
        shards,
        mesh=mesh,
        in_specs=(
            P("tm", "head"),
            P("tm", "head"),
            P("tm", "head"),
            P(None, "head"),
            P("tm", "head"),
        ),
        out_specs=(P("tm", "head"), P("tm", "head"), P("tm", "head"), P("tm", "head")),
        check_vma=False,
    )
```

profile of v0, /device:TPU:8, one launch (start us, length us, event | category | flops | bytes accessed | tf_op | source)
XLA Modules:
  0.0 762.1 jit_solution(17532904357043658640)
XLA Ops:
  9.7 1.9 fusion.33
  11.8 50.6 %all_gather.31 = f32[64,5,112]{2,1,0:T(8,128)} all-gather(f32[1,5,112]{2,1,0:T(8,128)S(1)} %all_gather.30), channel_id=1, replica_groups=mesh['tm'=64,'head'=4] {'tm'}, dimensions={0}, use_global_device_ids=true | all-gather | bytes 145600 | tf_op jit(solution)/shard_map/all_gather | solution.py:13
  62.6 1.5 broadcast_maximum_fusion
  64.1 4.7 multiply_reduce_fusion
  68.9 2.4 copy-done.1
  71.2 4.3 fusion.13
  75.6 13.2 %fusion.32 = f32[512,560]{0,1:T(8,128)} fusion(f32[512,2240]{0,1:T(8,128)} %all-gather.8.cloned.1.call-done, f32[2240,560]{0,1:T(8,128)} %param.12), kind=kOutput, calls=%fused_computation.53 | convolution fusion | flops 7707033600 | bytes 10752000 | tf_op jit(solution)/shard_map/dot_general | solution.py:49
  88.7 84.4 %all-gather.10.cloned.1.call-done = f32[320,112,112]{2,1,0:T(8,128)} async-done(((f32[5,112,112]{2,1,0:T(8,128)}), f32[320,112,112]{2,1,0:T(8,128)}) %all-gather.10.cloned.1.call-update) | async-done | bytes 16056336 | tf_op jit(solution)/shard_map/all_gather | solution.py:13
  175.1 2.8 multiply_reduce_fusion.1
  178.0 10.4 %convolution_bitcast_fusion = f32[2240,560]{0,1:T(8,128)} fusion(f32[512,560]{0,1:T(8,128)S(1)} %bitcast.112, f32[512,2240]{0,1:T(8,128)S(1)} %copy-done.6), kind=kOutput, calls=%fused_computation.5 | convolution fusion | flops 7707033600 | bytes 10752000 | tf_op jit(solution)/shard_map/dot_general | solution.py:88
  188.5 3.2 fusion.30
  192.9 2.2 broadcast_compare_fusion
  195.3 1.0 fusion.24
  196.4 199.6 %all-gather.3 = f32[64,5,112]{2,1,0:T(8,128)} all-gather(f32[1,5,112]{2,1,0:T(8,128)S(1)} %bitcast.121), channel_id=4, replica_groups=mesh['tm'=64,'head'=4] {'tm'}, dimensions={0}, use_global_device_ids=true | all-gather | bytes 145600 | tf_op jit(solution)/shard_map/all_gather | solution.py:13
  396.0 4.3 fusion.31
  400.3 3.3 fusion.1
  403.7 2.3 fusion.17
  406.0 6.6 fusion
  412.5 6.3 fusion.2
  418.8 118.7 %all-reduce.3.cloned.1.call-done = f32[2240,560]{0,1:T(8,128)} async-done(((f32[2240,560]{0,1:T(8,128)}), f32[2240,560]{0,1:T(8,128)}) %all-reduce.3.cloned.1.call-update) | async-done | bytes 5017616
  537.5 1.2 constant_dynamic-slice_fusion
  539.5 102.7 %all-gather.12.cloned.1.call-done = f32[320,112,112]{2,1,0:T(8,128)} async-done(((f32[5,112,112]{2,1,0:T(8,128)}), f32[320,112,112]{2,1,0:T(8,128)}) %all-gather.12.cloned.1.call-update) | async-done | bytes 16056336 | tf_op jit(solution)/shard_map/all_gather | solution.py:13
  642.2 107.2 %while.27 = (s32[]{:T(128)}, f32[5,112,112]{2,1,0:T(8,128)S(1)}, f32[5,112]{1,0:T(8,128)S(1)}, s32[]{:T(128)}, f32[64,5,112,112]{3,2,1,0:T(8,128)}, /*index=5*/f...) while((s32[]{:T(128)}, f32[5,112,112]{2,1,0:T(8,128)S(1)}, f32[5,112]{1,0:T(8,128)S(1)}, ...), condition=%wide.region_6.7_spmd, body=%wide.region_5.6_spmd.sunk | while | flops 63286 | bytes 759515 | solution.py:22
  642.2 1.0 bitcast_add_fusion.11
  643.9 1.0 bitcast_add_fusion.11
  645.6 1.0 bitcast_add_fusion.11
  647.3 1.0 bitcast_add_fusion.11
  649.0 1.0 bitcast_add_fusion.11
  650.7 1.0 bitcast_add_fusion.11
  652.4 1.0 bitcast_add_fusion.11
  749.4 3.5 convolution_add_fusion
  752.9 2.2 fusion.20
  (178 shorter events, 106.4 us)
Async XLA Ops:
  7.2 1.6 copy-start
  7.2 1.4 copy-start.10
  7.2 68.4 %all-gather.8.cloned.1.call-start = ((), (), s32[]{:S(2)}) async-start(), calls=%async_computation | async-start | bytes 5734400 | tf_op jit(solution)/shard_map/all_gather | solution.py:48
  7.9 165.2 %all-gather.10.cloned.1.call-start = ((), (), s32[]{:S(2)}) async-start(), calls=%async_computation.1 | async-start | bytes 18636800 | tf_op jit(solution)/shard_map/all_gather | solution.py:13
  8.7 1.0 copy-start.2
  11.7 525.8 %all-reduce.3.cloned.1.call-start = ((), (), s32[]{:S(2)}) async-start(), calls=%async_computation.3 | async-start | bytes 10321920
  62.5 1.6 copy-start.3
  68.9 2.4 copy-start.1
  173.9 1.3 copy-start.7
  175.1 2.8 copy-start.6
  188.4 3.3 copy-start.14
  188.4 453.8 %all-gather.12.cloned.1.call-start = ((), (), s32[]{:S(2)}) async-start(), calls=%async_computation.2 | async-start | bytes 18636800 | tf_op jit(solution)/shard_map/all_gather | solution.py:13
  192.9 2.2 copy-start.11
  195.2 200.8 %copy-start.8 = (f32[512,560]{0,1:T(8,128)S(1)}, f32[512,560]{0,1:T(8,128)}, u32[]{:S(2)}) copy-start(f32[512,560]{0,1:T(8,128)} %fusion.32) | copy-start | bytes 3440644
  396.0 4.3 copy-start.4
  400.3 3.3 copy-start.9
  403.6 8.9 %slice-start = ((s8[5242880]{0:T(1024)(128)(4,1)}), s8[4194304]{0:T(1024)(128)(4,1)S(1)}, s32[]{:S(2)}) async-start(s8[5242880]{0:T(1024)(128)(4,1)} %bitcast.95), calls=%async_computation.4 | async-start | bytes 8388608
  406.0 6.6 slice-start.1
  538.7 210.7 %copy-start.5 = (f32[512,560]{0,1:T(8,128)S(1)}, f32[512,560]{0,1:T(8,128)}, u32[]{:S(2)}) copy-start(f32[512,560]{0,1:T(8,128)} %copy-done.2) | copy-start | bytes 3440644
  749.4 3.5 copy-start.12
  749.4 3.5 copy-start.13
Sparse Core Ops, SparseCore 0:
  9.8 56.3 all-gather.7
  68.9 104.1 all-gather.9
  188.5 348.9 all-reduce.2
  540.1 102.0 all-gather.11
where the time goes:
time: 775 us; the launch traced here: 762 us
  waiting for transfers between devices  307 us (40%)
  blocking collectives  250 us (32%)
  other arithmetic  111 us (14%)
  matrix products  70.6 us (9%)
  between operations  15.1 us (2%)
  local copies, waits for them, and re-layouts  8.13 us (1%)
    all_gather x2, blocking collectives, prefix(): gathered = jax.tree.map(lambda a: lax.all_gather(a, axis), part)  250 us
    all_gather x2, waiting for transfers between devices, prefix(): gathered = jax.tree.map(lambda a: lax.all_gather(a, axis), part)  187 us
    unnamed x5, waiting for transfers between devices  119 us
    add x126, other arithmetic, add_pair(): return (earlier[0] + later[0], earlier[1] + later[1])  107 us
  transfers between devices with their start and end apart: 4, of which 3 were waited for; matrix products, arithmetic and copies ran while one was open for 8% of the time, Pallas kernels for 0%

commit v1 on v0

v1 whole, which is shorter than its diff:
```python
import functools

import jax
import jax.numpy as jnp
from jax import lax
from jax.experimental import pallas as pl
from jax.experimental.pallas import tpu as pltpu
from jax.sharding import Mesh, PartitionSpec as P


HD = 112
NH = 5
W = NH * HD
PADDED = 128
TOK = 512
BLK = 256
TM = ("x", "z", "c")
F32 = jnp.float32
BF16 = jnp.bfloat16
VMEM = pl.BlockSpec(memory_space=pltpu.VMEM)


def ring(n, step):
    return [(i, (i + step) % n) for i in range(n)]


def split(x):
    hi = x.astype(BF16)
    return hi, (x - hi.astype(F32)).astype(BF16)


def dot(a, b, cb):
    return lax.dot_general(a, b, (((1,), (cb,)), ((), ())), preferred_element_type=F32)


def mm(a, b, cb):
    rows = a[0].shape[0]
    both = dot(jnp.concatenate(a, 0), b[0], cb)
    return both[:rows] + both[rows:] + dot(a[0], b[1], cb)


def mm_feat(a, b):
    wide = dot(jnp.concatenate(a, 1), jnp.concatenate([b[0], b[0]], 0), 0)
    return wide + dot(a[0], b[1], 0)


def head(ref, h, extra=None):
    x = ref[h * HD : (h + 1) * HD, :]
    pad = jnp.zeros((PADDED - HD, x.shape[1]), F32)
    if extra is not None:
        row = lax.broadcasted_iota(jnp.int32, pad.shape, 0)
        pad = jnp.where(row == 0, extra, pad)
    return jnp.concatenate([x, pad], 0)


def feat(ref, h):
    return jnp.maximum(head(ref, h), 0.0)


def causal(x):
    row = lax.broadcasted_iota(jnp.int32, x.shape, 0)
    col = lax.broadcasted_iota(jnp.int32, x.shape, 1)
    return jnp.where(row <= col, x, 0.0)


def blk(pair, i):
    return tuple(a[:, i * BLK : (i + 1) * BLK] for a in pair)


def put_states(states, buf, rest, mine, other):
    for h in range(4):
        buf[h * HD : (h + 1) * HD, :] = states[h][:HD]
    buf[4 * HD : TOK, :] = states[4][: TOK - 4 * HD]
    rest[0:48, :] = states[4][TOK - 4 * HD : HD]
    rest[48:56, :] = jnp.zeros((8, 128), F32)
    for h in range(NH):
        rest[48 + h : 49 + h, :] = states[h][HD : HD + 1]
    for m in range(7):
        buf[56 * m : 56 * m + 56, HD:] = rest[:, 16 * m : 16 * m + 16]
    core = lax.axis_index("c")
    mine[...] = buf[pl.ds(pl.multiple_of(core * BLK, BLK), BLK), :]
    other[...] = buf[pl.ds(pl.multiple_of((1 - core) * BLK, BLK), BLK), :]


def get_states(own, far, buf, rest):
    core = lax.axis_index("c")
    buf[pl.ds(pl.multiple_of(core * BLK, BLK), BLK), :] = own[...]
    buf[pl.ds(pl.multiple_of((1 - core) * BLK, BLK), BLK), :] = far[...]
    rest[...] = jnp.zeros_like(rest)
    for m in range(7):
        rest[:, 16 * m : 16 * m + 16] = buf[56 * m : 56 * m + 56, HD:]
    keep = lax.broadcasted_iota(jnp.int32, (HD, 128), 1) < HD
    out = []
    for h in range(NH):
        if h < 4:
            rows = buf[h * HD : (h + 1) * HD, :]
        else:
            rows = jnp.concatenate([buf[4 * HD : TOK, :], rest[0:48, :]], 0)
        tail = jnp.concatenate([rest[48 + h : 49 + h, :], jnp.zeros((15, 128), F32)], 0)
        out.append(jnp.concatenate([jnp.where(keep, rows, 0.0), tail], 0))
    return out


def state_kernel(k, v, mine, other, buf, rest):
    states = [mm(split(head(v, h, 1.0)), split(feat(k, h)), 1) for h in range(NH)]
    put_states(states, buf, rest, mine, other)


def intra_kernel(q, k, v, numer):
    for h in range(NH):
        qs = split(feat(q, h))
        kt = split(feat(k, h).T)
        vs = split(head(v, h, 1.0))
        for t in range(2):
            total = None
            for s in range(t + 1):
                scores = mm_feat(tuple(a[s * BLK : (s + 1) * BLK] for a in kt), blk(qs, t))
                if s == t:
                    scores = causal(scores)
                part = mm(blk(vs, s), split(scores), 0)
                total = part if total is None else total + part
            numer[h, :, t * BLK : (t + 1) * BLK] = total


def attend_kernel(q, numer, own, far, att, inv, states, buf, rest):
    for h, st in enumerate(get_states(own, far, buf, rest)):
        states[h] = st
        total = numer[h] + mm_feat(split(st), split(feat(q, h)))
        one = 1.0 / (1.0 + total[HD : HD + 1])
        inv[h] = one
        att[h * HD : (h + 1) * HD, :] = total[:HD] * one


def weight_kernel(w, wh, wl):
    core, y = lax.axis_index("c"), lax.axis_index("head")
    for p in range(4):
        off = lax.rem(p - y + 4, 4)
        slot = jnp.where(off == 1, 2 - core, jnp.where(off == 3, 1 + core, jnp.where(off == 2, 3, 0)))
        wh[slot], wl[slot] = split(w[:, p * W : (p + 1) * W])


def grad_att_kernel(wh, wl, c0, c1, c2, out):
    total = None
    for slot, block in enumerate((c0, c1, c2)):
        part = mm((wh[slot], wl[slot]), split(block[...]), 0)
        total = part if total is None else total + part
    out[...] = total


def back_kernel(grad, wh, wl, c3, q, att, inv, gnum, mine, other, buf, rest, ga):
    ga[...] = grad[...] + mm((wh[3], wl[3]), split(c3[...]), 0)
    states = []
    for h in range(NH):
        g = ga[h * HD : (h + 1) * HD, :]
        den = -jnp.sum(g * att[h * HD : (h + 1) * HD, :], axis=0, keepdims=True)
        gn = head(ga, h, den) * inv[h]
        gnum[h] = gn
        states.append(mm(split(gn), split(feat(q, h)), 1))
    put_states(states, buf, rest, mine, other)


CUT = 3


def local_kernel(heads, q, k, v, gnum, states, *refs):
    base = heads[0] * HD
    fk, fv = refs[-2:]
    gq = refs[-3]
    if base:
        gq[:base, :] = refs[0][...]
    for h in heads:
        qs, ks = split(feat(q, h)), split(feat(k, h))
        kt = split(feat(k, h).T)
        vt = split(head(v, h, 1.0).T)
        gs = split(gnum[h])
        st = split(states[h].T)
        here = slice(h * HD, (h + 1) * HD)
        part = slice(h * HD - base, (h + 1) * HD - base)
        of_q = [mm_feat(st, blk(gs, t)) for t in range(2)]
        for s in range(2):
            of_k = of_v = None
            at = tuple(a[s * BLK : (s + 1) * BLK] for a in kt)
            vat = tuple(a[s * BLK : (s + 1) * BLK] for a in vt)
            for t in range(s, 2):
                scores, grads = mm_feat(at, blk(qs, t)), mm_feat(vat, blk(gs, t))
                if s == t:
                    scores, grads = causal(scores), causal(grads)
                scores, grads = split(scores), split(grads)
                of_q[t] = of_q[t] + mm(blk(ks, s), grads, 0)
                pk, pv = mm(blk(qs, t), grads, 1), mm(blk(gs, t), scores, 1)
                of_k = pk if of_k is None else of_k + pk
                of_v = pv if of_v is None else of_v + pv
            fk[part, s * BLK : (s + 1) * BLK] = of_k[:HD]
            fv[part, s * BLK : (s + 1) * BLK] = of_v[:HD]
        for t in range(2):
            cols = slice(t * BLK, (t + 1) * BLK)
            gq[here, cols] = jnp.where(q[here, cols] > 0, of_q[t][:HD], 0.0)


def final_kernel(k, v, fka, fva, fkb, fvb, own, far, gk, gv, buf, rest):
    for h, back in enumerate(get_states(own, far, buf, rest)):
        here = slice(h * HD, (h + 1) * HD)
        fk, fv, base = (fka, fva, 0) if h < CUT else (fkb, fvb, CUT * HD)
        part = slice(h * HD - base, (h + 1) * HD - base)
        of_k = mm_feat(split(back.T), split(head(v, h, 1.0)))[:HD] + fk[part, :]
        of_v = mm_feat(split(back), split(feat(k, h)))[:HD] + fv[part, :]
        gk[here, :] = jnp.where(k[here, :] > 0, of_k, 0.0)
        gv[here, :] = of_v


def sums_kernel(reverse, source, before, parts, sem):
    copy = pltpu.make_async_copy(source, parts, sem)
    copy.start()
    copy.wait()

    def one(i, total):
        k = 31 - i if reverse else i
        before[k] = total
        return total + parts[k]

    lax.fori_loop(0, 32, one, jnp.zeros((8, 128), F32), unroll=8)


def put_rows(block, mine, other, j):
    core = lax.axis_index("c")
    for z in range(8):
        pair = [block[70 * z + 35 * c : 70 * z + 35 * c + 35, :] for c in range(2)]
        for ref, one in ((mine, core == 0), (other, core == 1)):
            piece = jnp.where(one, pair[0], pair[1])
            for b in range(4):
                ref[j, z, 35 * b : 35 * b + 35, :] = piece[:, 128 * b : 128 * b + 128]
            ref[j, z, 140:160, :] = jnp.zeros((20, 128), F32)
            ref[j, z, 140:158, 0:48] = piece[0:18, 512:560]
            ref[j, z, 140:157, 64:112] = piece[18:35, 512:560]


def rows_kernel(c0, c1, c2, att, mine, other, buf):
    core = lax.axis_index("c")
    at = split(att[...])
    for j, block in ((0, c0), (2 - core, c1), (1 + core, c2)):
        buf[...] = mm(split(block[...]), at, 1)
        put_rows(buf, mine, other, j)


def rows_late_kernel(c3, att, mine, other, buf):
    buf[...] = mm(split(c3[...]), split(att[...]), 1)
    put_rows(buf, mine, other, 0)


def merge_kernel(e0, e1, l0, l1, to_a, to_b, keep_a, keep_b, sums):
    for j in range(3):
        sums[j + (j == 2)] = e0[j] + e1[j]
    sums[2] = l0[0] + l1[0]
    x, y = lax.axis_index("x"), lax.axis_index("head")
    side = 1 - 2 * lax.rem(x, 2)
    at = lambda p: lax.rem(p - y + 8, 4)
    lo, hi = slice(0, 4), slice(4, 8)
    for dst, place, pieces in (
        (to_a, lo, (x + side, x + 2)),
        (to_b, hi, (x - side, x + 2)),
        (keep_a, lo, (x - side, x)),
        (keep_b, hi, (x + side, x)),
    ):
        for i, p in enumerate(pieces):
            dst[i] = sums[at(p), place]


def step_kernel(keep_a, keep_b, got_a, got_b, send_a, send_b, own):
    send_a[...] = keep_a[0] + got_a[1]
    send_b[...] = keep_b[0] + got_b[1]
    own[0:4] = keep_a[1] + got_a[0]
    own[4:8] = keep_b[1] + got_b[0]


def plane_kernel(own, got_a, got_b, out):
    out[0:4] = own[0:4] + got_a[...]
    out[4:8] = own[4:8] + got_b[...]


def unpack_kernel(source, out, parts, sem):
    copy = pltpu.make_async_copy(source, parts, sem)
    copy.start()
    copy.wait()
    total = parts[0]
    for z in range(1, 8):
        total = total + parts[z]
    for b in range(4):
        out[:, 128 * b : 128 * b + 128] = total[35 * b : 35 * b + 35]
    out[0:18, 512:560] = total[140:158, 0:48]
    out[18:35, 512:560] = total[140:157, 64:112]


def call(kernel, outs, scratch, flops=0, hbm=False, room=6):
    shapes = tuple(jax.ShapeDtypeStruct(s, d) for s, d in outs)
    scratch = [pltpu.VMEM(s, F32) for s in scratch]
    if hbm:
        scratch.append(pltpu.SemaphoreType.DMA)
    where = pl.BlockSpec(memory_space=pltpu.HBM) if hbm else VMEM

    def run(*args):
        moved = sum(a.size * a.dtype.itemsize for a in (*args, *shapes))
        return pl.pallas_call(
            kernel,
            out_shape=shapes,
            in_specs=[where] * len(args),
            out_specs=(VMEM,) * len(shapes),
            scratch_shapes=scratch,
            compiler_params=pltpu.CompilerParams(
                vmem_limit_bytes=moved + moved // 4 + (room << 20)
            ),
            cost_estimate=pl.CostEstimate(
                flops=flops, bytes_accessed=moved, transcendentals=0
            ),
        )(*args)

    return run


def spread(a, axes):
    return lax.all_to_all(a, axes, 0, 0, tiled=True)


PAD = ((NH, PADDED, TOK), F32)
FLAT = ((W, TOK), F32)
HALF = ((BLK, 128), F32)
STATES = [(TOK, 128), (56, 128)]


def exclusive(mine, other, reverse):
    core = lax.axis_index("c")
    shape = (32, 8, 128)
    mine = mine.reshape(shape)
    other = lax.ppermute(other, "c", ring(2, 1)).reshape(shape)
    parts = spread(mine + other, ("x", "z"))
    (before,) = call(
        functools.partial(sums_kernel, reverse), [(shape, F32)], [shape], hbm=True
    )(parts)
    half = spread(before, ("x", "z"))
    late = (core == 0) if reverse else (core == 1)
    from_other = lax.ppermute(jnp.where(late, half, half + mine), "c", ring(2, 1))
    own = jnp.where(late, half + other, half)
    return own.reshape(BLK, 128), from_other.reshape(BLK, 128)


PAIRS_A = [(0, 1), (1, 0), (2, 3), (3, 2)]
PAIRS_B = [(1, 2), (2, 1), (3, 0), (0, 3)]


def scatter_rows(early, late):
    pair = ring(2, 1)
    got_e = lax.ppermute(early[1], "c", pair)
    got_l = lax.ppermute(late[1], "c", pair)
    half = ((2, 4, 160, 128), F32)
    to_a, to_b, keep_a, keep_b = call(merge_kernel, [half] * 4, [(4, 8, 160, 128)])(
        early[0], got_e, late[0], got_l
    )
    got_a = lax.ppermute(to_a, "x", PAIRS_A)
    got_b = lax.ppermute(to_b, "x", PAIRS_B)
    send_a, send_b, own = call(
        step_kernel, [((4, 160, 128), F32)] * 2 + [((8, 160, 128), F32)], []
    )(keep_a, keep_b, got_a, got_b)
    got_a = lax.ppermute(send_a, "x", PAIRS_B)
    got_b = lax.ppermute(send_b, "x", PAIRS_A)
    (plane,) = call(plane_kernel, [((8, 160, 128), F32)], [])(own, got_a, got_b)
    got = spread(plane, "z")
    return call(unpack_kernel, [((35, W), F32)], [(8, 160, 128)], hbm=True)(got)[0]


def shards(query_rows, key_rows, value_rows, out_weight, cotangent):
    q, k, v, w, c0 = (a.T for a in (query_rows, key_rows, value_rows, out_weight, cotangent))
    first = [((c, y), (c, (y + 1 - 2 * c) % 4)) for c in range(2) for y in range(4)]
    second = [((c, y), (c, (y - 1 + 2 * c) % 4)) for c in range(2) for y in range(4)]
    number = lambda pairs: [(a[0] * 4 + a[1], b[0] * 4 + b[1]) for a, b in pairs]
    c1 = lax.ppermute(c0, ("c", "head"), number(first))
    c2 = lax.ppermute(c0, ("c", "head"), number(second))
    c3 = lax.ppermute(c1, ("c", "head"), number(first))
    mine, other = call(state_kernel, [HALF] * 2, STATES)(k, v)
    (numer,) = call(intra_kernel, [PAD], [], 8 * 10**9)(q, k, v)
    wh, wl = call(weight_kernel, [((4, W, W), BF16)] * 2, [])(w)
    own, far = exclusive(mine, other, False)
    att, inv, states = call(
        attend_kernel, [FLAT, ((NH, 1, TOK), F32), ((NH, 128, 128), F32)], STATES
    )(q, numer, own, far)
    (grad,) = call(grad_att_kernel, [FLAT], [], 6 * 10**9)(wh, wl, c0, c1, c2)
    early = call(rows_kernel, [((3, 8, 160, 128), F32)] * 2, [(W, W)], 6 * 10**9)(c0, c1, c2, att)
    late = call(rows_late_kernel, [((1, 8, 160, 128), F32)] * 2, [(W, W)], 2 * 10**9)(c3, att)
    gnum, mine, other = call(back_kernel, [PAD, HALF, HALF], STATES + [(W, TOK)])(
        grad, wh, wl, c3, q, att, inv
    )
    own, far = exclusive(mine, other, True)
    few = lambda n: ((n * HD, TOK), F32)
    gq, fka, fva = call(
        functools.partial(local_kernel, range(CUT)), [few(CUT)] * 3, [], 9 * 10**9
    )(q, k, v, gnum, states)
    gq, fkb, fvb = call(
        functools.partial(local_kernel, range(CUT, NH)), [FLAT] + [few(NH - CUT)] * 2, [], 6 * 10**9
    )(q, k, v, gnum, states, gq)
    gk, gv = call(final_kernel, [FLAT] * 2, STATES)(k, v, fka, fva, fkb, fvb, own, far)
    return (gq.T, gk.T, gv.T, scatter_rows(early, late))


def solution(mesh):
    fine = Mesh(mesh.devices.reshape(4, 8, 2, 4), ("x", "z", "c", "head"))
    tokens = P(TM, "head")

    return jax.shard_map(
        shards,
        mesh=fine,
        in_specs=(tokens, tokens, tokens, P(None, "head"), tokens),
        out_specs=(tokens, tokens, tokens, tokens),
        check_vma=False,
    )
```

time: 775 us -> 164 us (0.21); the launches traced: 762 us -> 161 us
  waiting for transfers between devices: 307 us -> 44.3 us
  blocking collectives: 250 us -> 21.7 us
  other arithmetic: 111 us -> 2.67 us
  matrix products: 70.6 us -> 0 us
  Pallas kernels: 0 us -> 42.9 us
  starting transfers between devices: 0.16 us -> 32.8 us
  between operations: 15.1 us -> 1.21 us
    all_gather x2 -> x0, blocking collectives: 250 us -> none  [prefix(): gathered = jax.tree.map(lambda a: lax.all_gather(a, axis), part)]
    all_gather x3 -> x0, waiting for transfers between devices: 187 us -> none  [the longest x2 187 us: prefix(): gathered = jax.tree.map(lambda a: lax.all_gather(a, axis), part)]
    unnamed x5 -> x0, waiting for transfers between devices: 119 us -> none
    add x127 -> x2, other arithmetic: 107 us -> 0.68 us  [exclusive(): parts = spread(mine + other, ('x', 'z'))]
    dot_general x16 -> x0, matrix products: 70.6 us -> none  [the longest x1 13.2 us: shards(): jnp.dot(whole_grad, out_weight, precision=highest, preferred_element_type...]
    pallas_call x0 -> x17, Pallas kernels: none -> 42.9 us  [run(): pl.pallas_call(kernel, out_shape=shapes, in_specs=[where] * len(args), ou...]
    ppermute x0 -> x13, waiting for transfers between devices: none -> 23.2 us  [the longest x1 10.3 us: shards(): c1 = lax.ppermute(c0, ('c', 'head'), number(first))]
    all_to_all x0 -> x4, starting transfers between devices: none -> 22.8 us  [spread(): return lax.all_to_all(a, axes, 0, 0, tiled=True)]
  transfers between devices with their start and end apart: 4 -> 17, of which waited for: 3 -> 9; matrix products, arithmetic and copies ran while one was open for 8% -> 2% of each run, Pallas kernels for 0% -> 24%
where the time goes in v1:
time: 164 us; the launch traced here: 161 us
  waiting for transfers between devices  44.3 us (27%)
  Pallas kernels  42.9 us (26%)
  starting transfers between devices  32.8 us (20%)
  blocking collectives  21.7 us (13%)
  local copies, waits for them, and re-layouts  15.2 us (9%)
  other arithmetic  2.67 us (2%)
    pallas_call x17, Pallas kernels, run(): pl.pallas_call(kernel, out_shape=shapes, in_specs=[where] * len(args), ou...  42.9 us
    all_to_all x4, starting transfers between devices, spread(): return lax.all_to_all(a, axes, 0, 0, tiled=True)  22.8 us
    all_to_all x1, blocking collectives, spread(): return lax.all_to_all(a, axes, 0, 0, tiled=True)  21.7 us
    all_to_all x4, waiting for transfers between devices, spread(): return lax.all_to_all(a, axes, 0, 0, tiled=True)  21 us
    unnamed x58, local copies, waits for them, and re-layouts  15.2 us
    ppermute x1, waiting for transfers between devices, shards(): c1 = lax.ppermute(c0, ('c', 'head'), number(first))  10.3 us
    ppermute x1, waiting for transfers between devices, shards(): c3 = lax.ppermute(c1, ('c', 'head'), number(first))  9.82 us
  transfers between devices with their start and end apart: 17, of which 9 were waited for; matrix products, arithmetic and copies ran while one was open for 2% of the time, Pallas kernels for 24%

profile of v1, /device:TPU:8, one launch (start us, length us, event | category | flops | bytes accessed | tf_op | source)
XLA Modules:
  0.0 160.8 jit_solution(1453721326083503039)
XLA Ops:
  0.6 1.2 copy-done.1
  1.9 1.3 copy-done.3
  4.1 1.3 collective-permute-done.3
  5.5 21.7 %all_to_all.25.source = f32[32,8,128]{2,1,0:T(8,128)S(1)} all-to-all(f32[32,8,128]{2,1,0:T(8,128)S(1)} %bitcast_add_fusion.1), channel_id=1, replica_groups=mesh['x'=4,'z'=8,'c'=2,'head'=4] {'x','z'}, dimensions={0} | all-to-all | bytes 262144 | tf_op jit(solution)/shard_map/all_to_all | solution.py:320
  28.1 4.6 %all-to-all-start.1 = ((f32[32,8,128]{2,1,0:T(8,128)}), f32[32,8,128]{2,1,0:T(8,128)}, u32[]{:S(2)}, u32[]{:S(2)}) async-start(f32[32,8,128]{2,1,0:T(8,128)} %copy-done.15), calls=%async_computation.1 | async-start | bytes 262144 | tf_op jit(solution)/shard_map/all_to_all | solution.py:320
  32.6 1.7 %collective-permute-start = (f32[560,512]{1,0:T(8,128)}, f32[560,512]{1,0:T(8,128)}, u32[]{:S(2)}, u32[]{:S(2)}) collective-permute-start(f32[560,512]{1,0:T(8,128)} %bitcast.46), channel_id=1, source_target_pairs={{0,1},{1,2},{2,3},{3,0},{4,7},{5,4},{6,5},{7,6},{8,9},{9,10},{10,1... | collective-permute-start | bytes 3440648 | tf_op jit(solution)/shard_map/ppermute | solution.py:374
  34.7 8.2 %all-to-all-done.1 = f32[32,8,128]{2,1,0:T(8,128)} async-done(((f32[32,8,128]{2,1,0:T(8,128)}), f32[32,8,128]{2,1,0:T(8,128)}, u32[]{:S(2)}, u32[]{:S(2)}) %all-to-all-start.1) | async-done | bytes 131104 | tf_op jit(solution)/shard_map/all_to_all | solution.py:320
  44.2 4.0 %shard_map.86.numer = f32[5,128,512]{2,1,0:T(8,128)S(1)} custom-call(f32[560,512]{1,0:T(8,128)S(1)} %bitcast.29, f32[560,512]{1,0:T(8,128)S(1)} %bitcast.35, f32[560,512]{1,0:T(8,128)S(1)} %bitcast.40), custom_call_target="tpu_custom_call" | custom-call | flops 8000000000 | bytes 4751360 | tf_op jit(solution)/shard_map/pallas_call | solution.py:302
  49.8 10.3 %collective-permute-done.c1 = f32[560,512]{1,0:T(8,128)} collective-permute-done((f32[560,512]{1,0:T(8,128)}, f32[560,512]{1,0:T(8,128)}, u32[]{:S(2)}, u32[]{:S(2)}) %collective-permute-start) | collective-permute-done | bytes 1146912 | tf_op jit(solution)/shard_map/ppermute | solution.py:374
  60.4 6.3 %shard_map.95 = (f32[3,8,160,128]{3,2,1,0:T(8,128)S(1)}, f32[3,8,160,128]{3,2,1,0:T(8,128)S(1)}) custom-call(f32[560,512]{1,0:T(8,128)S(1)} %bitcast.48, f32[560,512]{1,0:T(8,128)} %collective-permute-done.c1, f32[560,512]{1,0:T(8,128)} %collective-permute-done.1.c2, f32[560,512]{1,0:T(8,128)S(1)} %get-tuple-element.37.att), custom_call_target="tpu_custom_call" | custom-call | flops 6000000000 | bytes 8519680 | tf_op jit(solution)/shard_map/pallas_call | solution.py:302
  66.9 9.8 %collective-permute-done.2.c3 = f32[560,512]{1,0:T(8,128)S(1)} collective-permute-done((f32[560,512]{1,0:T(8,128)}, f32[560,512]{1,0:T(8,128)S(1)}, u32[]{:S(2)}, u32[]{:S(2)}) %collective-permute-start.2) | collective-permute-done | bytes 1146912 | tf_op jit(solution)/shard_map/ppermute | solution.py:376
  76.7 1.7 %shard_map.96 = (f32[1,8,160,128]{3,2,1,0:T(8,128)S(1)}, f32[1,8,160,128]{3,2,1,0:T(8,128)S(1)}) custom-call(f32[560,512]{1,0:T(8,128)S(1)} %collective-permute-done.2.c3, f32[560,512]{1,0:T(8,128)S(1)} %get-tuple-element.37.att), custom_call_target="tpu_custom_call" | custom-call | flops 2000000000 | bytes 3604480 | tf_op jit(solution)/shard_map/pallas_call | solution.py:302
  78.5 1.7 %shard_map.84 = (bf16[4,560,560]{2,1,0:T(8,128)(2,1)S(1)}, bf16[4,560,560]{2,1,0:T(8,128)(2,1)S(1)}) custom-call(f32[560,2240]{1,0:T(8,128)S(1)} %bitcast.28), custom_call_target="tpu_custom_call" | custom-call | bytes 10035200 | tf_op jit(solution)/shard_map/pallas_call | solution.py:302
  80.6 1.5 shard_map.97
  83.7 1.7 %collective-permute-start.9 = (f32[2,4,160,128]{3,2,1,0:T(8,128)}, f32[2,4,160,128]{3,2,1,0:T(8,128)}, u32[]{:S(2)}, u32[]{:S(2)}) collective-permute-start(f32[2,4,160,128]{3,2,1,0:T(8,128)} %get-tuple-element.57), channel_id=1, source_target_pairs={{0,64},{64,0},{128,192},{192,128},{1,65},{65,1},{129,193},{193,129... | collective-permute-start | bytes 1966088 | tf_op jit(solution)/shard_map/ppermute | solution.py:357
  85.5 2.1 %collective-permute-start.10 = (f32[2,4,160,128]{3,2,1,0:T(8,128)}, f32[2,4,160,128]{3,2,1,0:T(8,128)}, u32[]{:S(2)}, u32[]{:S(2)}) collective-permute-start(f32[2,4,160,128]{3,2,1,0:T(8,128)} %get-tuple-element.58), channel_id=1, source_target_pairs={{64,128},{128,64},{192,0},{0,192},{65,129},{129,65},{193,1},{1,193... | collective-permute-start | bytes 1966088 | tf_op jit(solution)/shard_map/ppermute | solution.py:358
  87.6 5.8 %shard_map.85.grad = f32[560,512]{1,0:T(8,128)S(1)} custom-call(bf16[4,560,560]{2,1,0:T(8,128)(2,1)S(1)} %get-tuple-element.33.wh, bf16[4,560,560]{2,1,0:T(8,128)(2,1)S(1)} %get-tuple-element.34.wl, f32[560,512]{1,0:T(8,128)S(1)} %bitcast.49, f32[560,512]{1,0:T(8,128)} %collective-permute-done.c1, f32[560,512]{1,0:T(8,128)} %collective-permute-done.1.c2), custom_call_target="tpu_custom_call" | custom-call | flops 6000000000 | bytes 9605120 | tf_op jit(solution)/shard_map/pallas_call | solution.py:302
  93.4 2.4 %shard_map.90 = (f32[5,128,512]{2,1,0:T(8,128)S(1)}, f32[256,128]{1,0:T(8,128)S(1)}, f32[256,128]{1,0:T(8,128)S(1)}) custom-call(f32[560,512]{1,0:T(8,128)S(1)} %shard_map.85.grad, bf16[4,560,560]{2,1,0:T(8,128)(2,1)S(1)} %get-tuple-element.33.wh, bf16[4,560,560]{2,1,0:T(8,128)(2,1)S(1)} %get-tuple-element.34.wl, f32[560,512]{1,0:T(8,128)S(1)} %collective-permute-done.2.c3, ...), custom_call_target="tpu_custom_call" | custom-call | bytes 11188224 | tf_op jit(solution)/shard_map/pallas_call | solution.py:302
  96.9 1.3 collective-permute-done.5
  99.6 7.7 %all-to-all-start.2 = ((f32[32,8,128]{2,1,0:T(8,128)}), f32[32,8,128]{2,1,0:T(8,128)}, u32[]{:S(2)}, u32[]{:S(2)}) async-start(f32[32,8,128]{2,1,0:T(8,128)} %bitcast_add_fusion), calls=%async_computation.2 | async-start | bytes 262144 | tf_op jit(solution)/shard_map/all_to_all | solution.py:320
  109.5 2.2 %shard_map.98 = (f32[4,160,128]{2,1,0:T(8,128)}, f32[4,160,128]{2,1,0:T(8,128)}, f32[8,160,128]{2,1,0:T(8,128)S(1)}) custom-call(f32[2,4,160,128]{3,2,1,0:T(8,128)S(1)} %copy-done.7, f32[2,4,160,128]{3,2,1,0:T(8,128)S(1)} %copy-done.9, f32[2,4,160,128]{3,2,1,0:T(8,128)} %collective-permute-done.9.got_a, f32[2,4,160,128]{3,2,1,0:T(8,128)} %collective-permute-done.10.got_b), custom_call_target="tpu_custom_call" | custom-call | bytes 3932160 | tf_op jit(solution)/shard_map/pallas_call | solution.py:302
  112.5 3.0 %collective-permute-start.11 = (f32[4,160,128]{2,1,0:T(8,128)}, f32[4,160,128]{2,1,0:T(8,128)}, u32[]{:S(2)}, u32[]{:S(2)}) collective-permute-start(f32[4,160,128]{2,1,0:T(8,128)} %get-tuple-element.60), channel_id=1, source_target_pairs={{64,128},{128,64},{192,0},{0,192},{65,129},{129,65},{193,1},{1,193... | collective-permute-start | bytes 983048 | tf_op jit(solution)/shard_map/ppermute | solution.py:362
  115.7 2.2 %all-to-all-done.2.source = f32[32,8,128]{2,1,0:T(8,128)} async-done(((f32[32,8,128]{2,1,0:T(8,128)}), f32[32,8,128]{2,1,0:T(8,128)}, u32[]{:S(2)}, u32[]{:S(2)}) %all-to-all-start.2) | async-done | bytes 131104 | tf_op jit(solution)/shard_map/all_to_all | solution.py:320
  119.6 6.2 %all-to-all-start.3 = ((f32[32,8,128]{2,1,0:T(8,128)}), f32[32,8,128]{2,1,0:T(8,128)}, u32[]{:S(2)}, u32[]{:S(2)}) async-start(f32[32,8,128]{2,1,0:T(8,128)} %copy-done.16), calls=%async_computation.3 | async-start | bytes 262144 | tf_op jit(solution)/shard_map/all_to_all | solution.py:320
  128.9 7.3 %all-to-all-done.3 = f32[32,8,128]{2,1,0:T(8,128)} async-done(((f32[32,8,128]{2,1,0:T(8,128)}), f32[32,8,128]{2,1,0:T(8,128)}, u32[]{:S(2)}, u32[]{:S(2)}) %all-to-all-start.3) | async-done | bytes 131104 | tf_op jit(solution)/shard_map/all_to_all | solution.py:320
  136.2 4.2 %all-to-all-start.4 = ((f32[8,160,128]{2,1,0:T(8,128)}), f32[8,160,128]{2,1,0:T(8,128)}, u32[]{:S(2)}, u32[]{:S(2)}) async-start(f32[8,160,128]{2,1,0:T(8,128)} %copy-done.5), calls=%async_computation.4 | async-start | bytes 1310720 | tf_op jit(solution)/shard_map/all_to_all | solution.py:320
  140.4 1.3 copy-done.18
  142.7 5.0 %shard_map.91 = (f32[336,512]{1,0:T(8,128)S(1)}, f32[336,512]{1,0:T(8,128)S(1)}, f32[336,512]{1,0:T(8,128)S(1)}) custom-call(f32[560,512]{1,0:T(8,128)S(1)} %bitcast.32, f32[560,512]{1,0:T(8,128)S(1)} %bitcast.36, f32[560,512]{1,0:T(8,128)S(1)} %bitcast.41, f32[5,128,512]{2,1,0:T(8,128)S(1)} %copy-done.18, f32[5,128,128]{2,1,0:T(8,128)S(1)} %copy-done.22), custom_call_target="tpu_custom_call" | custom-call | flops 8999999488 | bytes 7143424 | tf_op jit(solution)/shard_map/pallas_call | solution.py:302
  148.8 4.3 %shard_map.92 = (f32[560,512]{1,0:T(8,128)}, f32[224,512]{1,0:T(8,128)S(1)}, f32[224,512]{1,0:T(8,128)S(1)}) custom-call(f32[560,512]{1,0:T(8,128)S(1)} %bitcast.33, f32[560,512]{1,0:T(8,128)S(1)} %bitcast.37, f32[560,512]{1,0:T(8,128)S(1)} %bitcast.42, f32[5,128,512]{2,1,0:T(8,128)S(1)} %copy-done.19, f32[5,128,128]{2,1,0:T(8,128)S(1)} %copy-done.23, ...), custom_call_target="tpu_custom_call" | custom-call | flops 6000000000 | bytes 7831552 | tf_op jit(solution)/shard_map/pallas_call | solution.py:302
  153.0 2.4 %shard_map.94 = (f32[560,512]{1,0:T(8,128)}, f32[560,512]{1,0:T(8,128)}) custom-call(f32[560,512]{1,0:T(8,128)S(1)} %bitcast.38, f32[560,512]{1,0:T(8,128)S(1)} %bitcast.43, f32[336,512]{1,0:T(8,128)S(1)} %get-tuple-element.43.fka, f32[336,512]{1,0:T(8,128)S(1)} %get-tuple-element.44.fva, f32[224,512]{1,0:T(8,128)S(1)} %get-tuple-element.45.fkb, ...), custom_call_target="tpu_custom_call" | custom-call | bytes 7143424 | tf_op jit(solution)/shard_map/pallas_call | solution.py:302
  155.4 3.3 %all-to-all-done.4.source = f32[8,160,128]{2,1,0:T(8,128)} async-done(((f32[8,160,128]{2,1,0:T(8,128)}), f32[8,160,128]{2,1,0:T(8,128)}, u32[]{:S(2)}, u32[]{:S(2)}) %all-to-all-start.4) | async-done | bytes 655392 | tf_op jit(solution)/shard_map/all_to_all | solution.py:320
  158.8 1.8 %shard_map.100 = f32[35,560]{1,0:T(8,128)} custom-call(f32[8,160,128]{2,1,0:T(8,128)} %all-to-all-done.4.source), custom_call_target="tpu_custom_call" | custom-call | bytes 733760 | tf_op jit(solution)/shard_map/pallas_call | solution.py:302
  (83 shorter events, 19.9 us)
Async XLA Ops:
  0.6 1.3 copy-start.1
  3.2 41.0 %copy-start.2 = (f32[512,560]{0,1:T(8,128)S(1)}, f32[512,560]{0,1:T(8,128)}, u32[]{:S(2)}) copy-start(f32[512,560]{0,1:T(8,128)} %param.6) | copy-start | bytes 3440644
  3.2 41.0 %copy-start.4 = (f32[512,560]{0,1:T(8,128)S(1)}, f32[512,560]{0,1:T(8,128)}, u32[]{:S(2)}) copy-start(f32[512,560]{0,1:T(8,128)} %param.7) | copy-start | bytes 3440644
  4.0 1.5 copy-start.14
  4.0 40.2 %copy-start = (f32[512,560]{0,1:T(8,128)S(1)}, f32[512,560]{0,1:T(8,128)}, u32[]{:S(2)}) copy-start(f32[512,560]{0,1:T(8,128)} %param.5) | copy-start | bytes 3440644
  4.0 1.4 collective-permute-start.3
  5.4 21.8 %copy-start.26 = (f32[256,128]{1,0:T(8,128)}, f32[256,128]{1,0:T(8,128)S(1)}, u32[]{:S(2)}) copy-start(f32[256,128]{1,0:T(8,128)S(1)} %collective-permute-done.3) | copy-start | bytes 393220
  28.1 14.9 %all-to-all-start.1 = ((f32[32,8,128]{2,1,0:T(8,128)}), f32[32,8,128]{2,1,0:T(8,128)}, u32[]{:S(2)}, u32[]{:S(2)}) async-start(f32[32,8,128]{2,1,0:T(8,128)} %copy-done.15), calls=%async_computation.1 | async-start | bytes 262144 | tf_op jit(solution)/shard_map/all_to_all | solution.py:320
  32.6 27.4 %collective-permute-start = (f32[560,512]{1,0:T(8,128)}, f32[560,512]{1,0:T(8,128)}, u32[]{:S(2)}, u32[]{:S(2)}) collective-permute-start(f32[560,512]{1,0:T(8,128)} %bitcast.46), channel_id=1, source_target_pairs={{0,1},{1,2},{2,3},{3,0},{4,7},{5,4},{6,5},{7,6},{8,9},{9,10},{10,1... | collective-permute-start | bytes 3440648 | tf_op jit(solution)/shard_map/ppermute | solution.py:374
  34.3 26.1 %collective-permute-start.1 = (f32[560,512]{1,0:T(8,128)}, f32[560,512]{1,0:T(8,128)}, u32[]{:S(2)}, u32[]{:S(2)}) collective-permute-start(f32[560,512]{1,0:T(8,128)} %bitcast.47), channel_id=1, source_target_pairs={{0,3},{1,0},{2,1},{3,2},{4,5},{5,6},{6,7},{7,4},{8,11},{9,8},{10,9... | collective-permute-start | bytes 3440648 | tf_op jit(solution)/shard_map/ppermute | solution.py:375
  44.0 4.2 %collective-permute-start.4 = (f32[32,8,128]{2,1,0:T(8,128)S(1)}, f32[32,8,128]{2,1,0:T(8,128)S(1)}, u32[]{:S(2)}, u32[]{:S(2)}) collective-permute-start(f32[32,8,128]{2,1,0:T(8,128)S(1)} %get-tuple-element.64), channel_id=1, source_target_pairs={{0,4},{4,0},{1,5},{5,1},{2,6},{6,2},{3,7},{7,3},{8,12},{12,8},{9,1... | collective-permute-start | bytes 393224 | tf_op jit(solution)/shard_map/ppermute | solution.py:340
  44.2 16.2 %copy-start.20 = (f32[512,560]{0,1:T(8,128)S(1)}, f32[512,560]{0,1:T(8,128)}, u32[]{:S(2)}) copy-start(f32[512,560]{0,1:T(8,128)} %param.9) | copy-start | bytes 3440644
  48.3 30.2 %slice-start = ((s8[5160960]{0:T(1024)(128)(4,1)}), s8[4194304]{0:T(1024)(128)(4,1)S(1)}, s32[]{:S(2)}) async-start(s8[5160960]{0:T(1024)(128)(4,1)} %bitcast.26), calls=%async_computation.5 | async-start | bytes 8388608
  60.1 16.6 %collective-permute-start.2 = (f32[560,512]{1,0:T(8,128)}, f32[560,512]{1,0:T(8,128)S(1)}, u32[]{:S(2)}, u32[]{:S(2)}) collective-permute-start(f32[560,512]{1,0:T(8,128)} %collective-permute-done.c1), channel_id=1, source_target_pairs={{0,1},{1,2},{2,3},{3,0},{4,7},{5,4},{6,5},{7,6},{8,9},{9,10},{10,1... | collective-permute-start | bytes 3440648 | tf_op jit(solution)/shard_map/ppermute | solution.py:376
  60.4 18.1 %slice-start.1 = ((s8[5160960]{0:T(1024)(128)(4,1)}), s8[966656]{0:T(1024)(128)(4,1)S(1)}, s32[]{:S(2)}) async-start(s8[5160960]{0:T(1024)(128)(4,1)} %bitcast.26), calls=%async_computation.6 | async-start | bytes 1933312
  66.6 14.0 %collective-permute-start.7 = (f32[3,8,160,128]{3,2,1,0:T(8,128)S(1)}, f32[3,8,160,128]{3,2,1,0:T(8,128)S(1)}, u32[]{:S(2)}, u32[]{:S(2)}) collective-permute-start(f32[3,8,160,128]{3,2,1,0:T(8,128)S(1)} %get-tuple-element.52), channel_id=1, source_target_pairs={{0,4},{4,0},{1,5},{5,1},{2,6},{6,2},{3,7},{7,3},{8,12},{12,8},{9,1... | collective-permute-start | bytes 5898248 | tf_op jit(solution)/shard_map/ppermute | solution.py:351
  78.4 2.2 %collective-permute-start.8 = (f32[1,8,160,128]{3,2,1,0:T(8,128)S(1)}, f32[1,8,160,128]{3,2,1,0:T(8,128)S(1)}, u32[]{:S(2)}, u32[]{:S(2)}) collective-permute-start(f32[1,8,160,128]{3,2,1,0:T(8,128)S(1)} %get-tuple-element.54), channel_id=1, source_target_pairs={{0,4},{4,0},{1,5},{5,1},{2,6},{6,2},{3,7},{7,3},{8,12},{12,8},{9,1... | collective-permute-start | bytes 1966088 | tf_op jit(solution)/shard_map/ppermute | solution.py:352
  83.7 23.6 %collective-permute-start.9 = (f32[2,4,160,128]{3,2,1,0:T(8,128)}, f32[2,4,160,128]{3,2,1,0:T(8,128)}, u32[]{:S(2)}, u32[]{:S(2)}) collective-permute-start(f32[2,4,160,128]{3,2,1,0:T(8,128)} %get-tuple-element.57), channel_id=1, source_target_pairs={{0,64},{64,0},{128,192},{192,128},{1,65},{65,1},{129,193},{193,129... | collective-permute-start | bytes 1966088 | tf_op jit(solution)/shard_map/ppermute | solution.py:357
  85.5 21.9 %collective-permute-start.10 = (f32[2,4,160,128]{3,2,1,0:T(8,128)}, f32[2,4,160,128]{3,2,1,0:T(8,128)}, u32[]{:S(2)}, u32[]{:S(2)}) collective-permute-start(f32[2,4,160,128]{3,2,1,0:T(8,128)} %get-tuple-element.58), channel_id=1, source_target_pairs={{64,128},{128,64},{192,0},{0,192},{65,129},{129,65},{193,1},{1,193... | collective-permute-start | bytes 1966088 | tf_op jit(solution)/shard_map/ppermute | solution.py:358
  96.9 1.4 copy-start.12
  96.9 1.3 collective-permute-start.5
  99.6 18.4 %all-to-all-start.2 = ((f32[32,8,128]{2,1,0:T(8,128)}), f32[32,8,128]{2,1,0:T(8,128)}, u32[]{:S(2)}, u32[]{:S(2)}) async-start(f32[32,8,128]{2,1,0:T(8,128)} %bitcast_add_fusion), calls=%async_computation.2 | async-start | bytes 262144 | tf_op jit(solution)/shard_map/all_to_all | solution.py:320
  112.5 13.3 %collective-permute-start.11 = (f32[4,160,128]{2,1,0:T(8,128)}, f32[4,160,128]{2,1,0:T(8,128)}, u32[]{:S(2)}, u32[]{:S(2)}) collective-permute-start(f32[4,160,128]{2,1,0:T(8,128)} %get-tuple-element.60), channel_id=1, source_target_pairs={{64,128},{128,64},{192,0},{0,192},{65,129},{129,65},{193,1},{1,193... | collective-permute-start | bytes 983048 | tf_op jit(solution)/shard_map/ppermute | solution.py:362
  115.5 10.3 %collective-permute-start.12 = (f32[4,160,128]{2,1,0:T(8,128)}, f32[4,160,128]{2,1,0:T(8,128)}, u32[]{:S(2)}, u32[]{:S(2)}) collective-permute-start(f32[4,160,128]{2,1,0:T(8,128)} %get-tuple-element.61), channel_id=1, source_target_pairs={{0,64},{64,0},{128,192},{192,128},{1,65},{65,1},{129,193},{193,129... | collective-permute-start | bytes 983048 | tf_op jit(solution)/shard_map/ppermute | solution.py:363
  119.6 16.6 %all-to-all-start.3 = ((f32[32,8,128]{2,1,0:T(8,128)}), f32[32,8,128]{2,1,0:T(8,128)}, u32[]{:S(2)}, u32[]{:S(2)}) async-start(f32[32,8,128]{2,1,0:T(8,128)} %copy-done.16), calls=%async_computation.3 | async-start | bytes 262144 | tf_op jit(solution)/shard_map/all_to_all | solution.py:320
  136.2 22.6 %all-to-all-start.4 = ((f32[8,160,128]{2,1,0:T(8,128)}), f32[8,160,128]{2,1,0:T(8,128)}, u32[]{:S(2)}, u32[]{:S(2)}) async-start(f32[8,160,128]{2,1,0:T(8,128)} %copy-done.5), calls=%async_computation.4 | async-start | bytes 1310720 | tf_op jit(solution)/shard_map/all_to_all | solution.py:320
  140.4 1.3 copy-start.18
  142.7 5.0 %copy-start.13 = (f32[256,128]{1,0:T(8,128)S(1)}, f32[256,128]{1,0:T(8,128)}, u32[]{:S(2)}) copy-start(f32[256,128]{1,0:T(8,128)} %copy-done.12) | copy-start | bytes 393220
  142.7 5.0 %copy-start.25 = (f32[256,128]{1,0:T(8,128)S(1)}, f32[256,128]{1,0:T(8,128)}, u32[]{:S(2)}) copy-start(f32[256,128]{1,0:T(8,128)} %copy-done.24) | copy-start | bytes 393220
  142.7 6.1 %copy-start.19 = (f32[5,128,512]{2,1,0:T(8,128)S(1)}, f32[5,128,512]{2,1,0:T(8,128)}, u32[]{:S(2)}) copy-start(f32[5,128,512]{2,1,0:T(8,128)} %copy-done.17) | copy-start | bytes 3932164
  142.7 6.1 %copy-start.23 = (f32[5,128,128]{2,1,0:T(8,128)S(1)}, f32[5,128,128]{2,1,0:T(8,128)}, u32[]{:S(2)}) copy-start(f32[5,128,128]{2,1,0:T(8,128)} %copy-done.21) | copy-start | bytes 983044
  148.7 4.4 %collective-permute-start.6 = (f32[32,8,128]{2,1,0:T(8,128)S(1)}, f32[32,8,128]{2,1,0:T(8,128)S(1)}, u32[]{:S(2)}, u32[]{:S(2)}) collective-permute-start(f32[32,8,128]{2,1,0:T(8,128)S(1)} %get-tuple-element.62), channel_id=1, source_target_pairs={{0,4},{4,0},{1,5},{5,1},{2,6},{6,2},{3,7},{7,3},{8,12},{12,8},{9,1... | collective-permute-start | bytes 393224 | tf_op jit(solution)/shard_map/ppermute | solution.py:340
  (14 other events, 12.7 us)
